TPU v7x, 32 devices: a whole 2x2x4 slice. The times are simulated.
32 devices in a mesh: grp: 1, date: 4 (over y, x), shard: 8 (over z, core).
Axes of the slice: x: 2, y: 2, z: 4, core: 2. Of those that a mesh axis runs over, the one named last changes fastest.
Arguments:
- echo_spectra: bfloat16 [4, 2, 128, 8192], P(('grp', 'date'), None, 'shard'), may hold values from -6 to 6
- range_reference: float32 [2, 8192], replicated, may hold values from -5 to 5
- azimuth_reference: bfloat16 [2, 128, 8192], P(None, None, 'shard'), may hold values from -5 to 5
- block_owner: int32 [4, 64], P(('grp', 'date')), may hold values from 0 to 7, as said below
- block_slot: int32 [4, 64], P(('grp', 'date')), may hold values from 0 to 15, as said below
- kernel_index: int32 [4, 64], P(('grp', 'date')), may hold values from 0 to 7
Outputs:
- filtered: bfloat16 [4, 128, 2, 2, 128, 128], P(('grp', 'date'), 'shard')
Inputs may be any that keep to these rules, and one draw needn't show every extreme that they name: `block_owner`: every date carries the same owners (the stack is coregistered onto one map grid). Within a date, the 8 blocks of one range-column group name any one owner at most 2 times, and some group names some owner exactly 2 times; every owner is named by at most 16 blocks, and some owner by exactly 16. `block_slot`: every date carries the same slots. Within a date, blocks that name the same owner have distinct slots.
All inputs are finite; a program needn't handle non-finite values.
Results may differ from a plain program's by a relative error of at most 0.017.
Values may be sent and summed in bfloat16 or wider, within the bound.
A program may use at most 128 MiB of HBM per device.

v0:
```python
import math

import jax
import jax.numpy as jnp
from jax import lax
from jax.sharding import PartitionSpec as P

RNG = 8192
RSPLIT = 64
BLK = 128
NSUB = 8
BLK_DEV = 8


def passed_along(value, axis, steps):
    count = lax.axis_size(axis)
    pairs = [(source, (source + steps) % count) for source in range(count)]
    return lax.ppermute(value, axis, pairs)


def dft_block(size, sign):
    index = jnp.arange(size, dtype=jnp.int32)
    phase = index[:, None] * index[None, :] % size
    angle = 2.0 * math.pi / size * phase.astype(jnp.float32)
    scale = 1.0 / math.sqrt(size)
    cosine = jnp.cos(angle) * scale
    sine = sign * jnp.sin(angle) * scale
    table = jnp.stack([jnp.stack([cosine, -sine]), jnp.stack([sine, cosine])])
    return jnp.transpose(table, (0, 2, 1, 3)).astype(jnp.bfloat16)


def twiddle(first_len, second_len, total):
    left = jnp.arange(first_len, dtype=jnp.int32)
    right = jnp.arange(second_len, dtype=jnp.int32)
    phase = left[:, None] * right[None, :] % total
    angle = 2.0 * math.pi / total * phase.astype(jnp.float32)
    return (jnp.cos(angle), jnp.sin(angle))


def kernel_table():
    offset = (jnp.arange(NSUB, dtype=jnp.float32) + 0.5) / NSUB
    cells = jnp.arange(BLK, dtype=jnp.float32)
    dist = cells[None, None, :] - cells[None, :, None] - offset[:, None, None]
    window = jnp.where(jnp.abs(dist) < 4.0, 0.5 + 0.5 * jnp.cos(math.pi * dist / 4.0), 0.0)
    return (jnp.sinc(dist) * window).astype(jnp.bfloat16)


def bdot(form, left, right):
    return jnp.einsum(form, left, right, preferred_element_type=jnp.float32)


def range_compress(spectra, reference):
    real_in = spectra[0].astype(jnp.float32)
    imag_in = spectra[1].astype(jnp.float32)
    matched = jnp.stack(
        [
            real_in * reference[0] + imag_in * reference[1],
            imag_in * reference[0] - real_in * reference[1],
        ]
    ).astype(jnp.bfloat16)
    count = spectra.shape[1]
    outer_len = RSPLIT
    inner_len = RNG // RSPLIT
    shaped = matched.reshape(2, count, outer_len, inner_len)
    section = bdot("cnek,epkb->cpnb", dft_block(outer_len, 1), shaped)
    twc, tws = twiddle(outer_len, inner_len, RNG)
    first = jnp.stack(
        [section[0] * twc - section[1] * tws, section[0] * tws + section[1] * twc]
    ).astype(jnp.bfloat16)
    second = bdot("cmek,epnk->cpmn", dft_block(inner_len, 1), first)
    return second.reshape(2, count, RNG).astype(jnp.bfloat16)


def azimuth_focus(columns, reference):
    count = columns.shape[1]
    doppler = bdot("cuep,epk->cuk", dft_block(count, -1), columns)
    ref_re = reference[0].astype(jnp.float32)
    ref_im = reference[1].astype(jnp.float32)
    shaped = jnp.stack(
        [doppler[0] * ref_re - doppler[1] * ref_im, doppler[0] * ref_im + doppler[1] * ref_re]
    ).astype(jnp.bfloat16)
    return bdot("cuep,epk->cuk", dft_block(count, 1), shaped).astype(jnp.bfloat16)


def resample(blocks, kinds):
    count = blocks.shape[0]
    picker = (kinds[:, None] == jnp.arange(NSUB, dtype=jnp.int32)[None, :]).astype(jnp.bfloat16)
    table = kernel_table().reshape(NSUB, BLK * BLK)
    kernels = (
        jnp.dot(picker, table, preferred_element_type=jnp.float32)
        .astype(jnp.bfloat16)
        .reshape(count, BLK, BLK)
    )
    return bdot("nij,ncjk->ncik", kernels, blocks).astype(jnp.bfloat16)


def cross(first, second):
    fre = first[:, 0].astype(jnp.float32)
    fim = first[:, 1].astype(jnp.float32)
    sre = second[:, 0].astype(jnp.float32)
    sim = second[:, 1].astype(jnp.float32)
    return jnp.stack([fre * sre + fim * sim, fim * sre - fre * sim], axis=1)


def goldstein(patches):
    forward = dft_block(BLK, -1)
    backward = dft_block(BLK, 1)
    rows = bdot("cuei,npeij->npcuj", forward, patches).astype(jnp.bfloat16)
    spectrum = bdot("npeuj,cvej->npcuv", rows, forward)
    power = spectrum[:, :, 0] ** 2 + spectrum[:, :, 1] ** 2
    smooth = jnp.zeros_like(power)
    for down in (-1, 0, 1):
        for across in (-1, 0, 1):
            smooth = smooth + jnp.roll(power, (down, across), axis=(-2, -1))
    smooth = smooth / 9.0
    level = jnp.mean(smooth, axis=(-2, -1), keepdims=True)
    weight = jnp.sqrt(jnp.sqrt(smooth / (level + 1e-06)))
    weighted = (spectrum * weight[:, :, None]).astype(jnp.bfloat16)
    back = bdot("cuei,npeij->npcuj", backward, weighted).astype(jnp.bfloat16)
    return bdot("npeuj,cvej->npcuv", back, backward).astype(jnp.bfloat16)


def body(echo_spectra, range_reference, azimuth_reference, block_owner, block_slot, kernel_index):
    shards = lax.axis_size("shard")
    most = max(2, 2 * BLK_DEV // shards)
    capacity = min(2 * BLK_DEV, shards * most)
    outgoing = shards * most
    compressed = range_compress(echo_spectra[0], range_reference)
    columns = lax.all_to_all(compressed, "shard", split_axis=2, concat_axis=1, tiled=True)
    image = azimuth_focus(columns, azimuth_reference)
    row_blocks = image.shape[1] // BLK
    col_blocks = image.shape[2] // BLK
    blocks = image.reshape(2, row_blocks, BLK, col_blocks, BLK)
    blocks = jnp.transpose(blocks, (1, 3, 0, 2, 4)).reshape(BLK_DEV, 2, BLK, BLK)
    owners = block_owner[0]
    slots = block_slot[0]
    kinds = kernel_index[0]
    total = owners.shape[0]
    me_index = lax.axis_index("shard")
    numbers = jnp.arange(total, dtype=jnp.int32)
    sender = numbers // BLK_DEV
    earlier = (
        (sender[:, None] == sender[None, :])
        & (owners[:, None] == owners[None, :])
        & (numbers[None, :] < numbers[:, None])
    )
    rank = jnp.sum(earlier.astype(jnp.int32), axis=1)
    target = owners * most + rank
    my_target = lax.dynamic_slice_in_dim(target, me_index * BLK_DEV, BLK_DEV)
    chooser = (my_target[None, :] == jnp.arange(outgoing, dtype=jnp.int32)[:, None]).astype(
        jnp.bfloat16
    )
    outbox = bdot("en,nxyz->exyz", chooser, blocks).astype(jnp.bfloat16)
    outbox = outbox.reshape(shards, most, 2, BLK, BLK)
    inbox = lax.all_to_all(outbox, "shard", split_axis=0, concat_axis=0, tiled=True).reshape(
        outgoing, 2, BLK, BLK
    )
    entry = sender * most + rank
    hits = owners == me_index
    slot_hit = (slots[None, :] == jnp.arange(capacity, dtype=jnp.int32)[:, None]) & hits[None, :]
    entry_hit = entry[:, None] == jnp.arange(outgoing, dtype=jnp.int32)[None, :]
    placing = jnp.dot(slot_hit.astype(jnp.float32), entry_hit.astype(jnp.float32)).astype(
        jnp.bfloat16
    )
    tile = bdot("qe,exyz->qxyz", placing, inbox).astype(jnp.bfloat16)
    slot_kinds = jnp.sum(slot_hit.astype(jnp.int32) * kinds[None, :], axis=1)
    tile = resample(tile, slot_kinds)
    following = passed_along(tile, "date", -1)
    second = passed_along(tile, "date", -2)
    pairs = jnp.stack([cross(tile, following), cross(tile, second)], axis=1).astype(jnp.bfloat16)
    return goldstein(pairs)[None]


def solution(mesh):
    in_specs = (
        P(("grp", "date"), None, "shard", None),
        P(),
        P(None, None, "shard"),
        P(("grp", "date"), None),
        P(("grp", "date"), None),
        P(("grp", "date"), None),
    )
    out_specs = P(("grp", "date"), "shard", None, None, None, None)
    return jax.shard_map(body, mesh=mesh, in_specs=in_specs, out_specs=out_specs, check_vma=False)
```

profile of v0, /device:TPU:2, one launch (start us, length us, event | category | flops | bytes accessed | tf_op | source)
XLA Modules:
  0.0 187.8 jit_solution(73576553824263236)
XLA Ops:
  3.8 5.6 %copy.128 = bf16[2,16,128,64]{1,0,3,2:T(2,128)(2,1)} copy(bf16[2,16,128,64]{2,3,0,1:T(8,128)(2,1)S(1)} %fusion.38) | data formatting | bytes 1048576 | tf_op jit(solution)/shard_map/convert_element_type | solution.py:71
  9.3 6.5 %reshape.594 = bf16[8,2,16384]{2,1,0:T(2,128)(2,1)} reshape(bf16[8192,2,16]{2,1,0:T(2,128)(2,1)} %bitcast.278) | data formatting | bytes 1048576
  15.8 4.9 %all-to-all-start = ((bf16[8,2,16384]{2,1,0:T(2,128)(2,1)}), bf16[8,2,16384]{2,1,0:T(2,128)(2,1)S(1)}, u32[]{:S(2)}, u32[]{:S(2)}) async-start(bf16[8,2,16384]{2,1,0:T(2,128)(2,1)} %reshape.594), calls=%async_computation | async-start | bytes 1048576 | tf_op jit(solution)/shard_map/all_to_all | solution.py:129
  21.0 15.0 %all-to-all-done = bf16[8,2,16384]{2,1,0:T(2,128)(2,1)S(1)} async-done(((bf16[8,2,16384]{2,1,0:T(2,128)(2,1)}), bf16[8,2,16384]{2,1,0:T(2,128)(2,1)S(1)}, u32[]{:S(2)}, u32[]{:S(2)}) %all-to-all-start) | async-done | bytes 524320 | tf_op jit(solution)/shard_map/all_to_all | solution.py:129
  36.0 4.1 %reshape.595 = bf16[8192,2,16]{2,1,0:T(2,128)(2,1)} reshape(bf16[8,2,16384]{2,1,0:T(2,128)(2,1)S(1)} %all-to-all-done) | data formatting | bytes 1048576
  40.1 9.0 %copy.130 = bf16[2,16,8,1024]{3,1,2,0:T(8,128)(2,1)S(1)} copy(bf16[2,16,8,1024]{1,0,3,2:T(2,128)(2,1)} %bitcast.279) | data formatting | bytes 1048576 | tf_op jit(solution)/shard_map/all_to_all | solution.py:129
  50.5 2.0 %copy.79 = bf16[8,2,2,128,128]{4,1,3,2,0:T(2,128)(2,1)} copy(bf16[8,2,2,128,128]{4,1,0,3,2:T(2,128)(2,1)S(1)} %bitcast.281) | data formatting | bytes 2097152 | tf_op jit(solution)/shard_map/reshape | solution.py:154
  52.5 3.6 %all-to-all-start.1 = ((bf16[8,2,2,128,128]{4,1,3,2,0:T(2,128)(2,1)}), bf16[8,2,2,128,128]{4,1,3,2,0:T(2,128)(2,1)S(1)}, u32[]{:S(2)}, u32[]{:S(2)}) async-start(bf16[8,2,2,128,128]{4,1,3,2,0:T(2,128)(2,1)} %copy.79), calls=%async_computation.1 | async-start | bytes 2097152 | tf_op jit(solution)/shard_map/all_to_all | solution.py:155
  56.3 2.8 %fusion.39 = bf16[2,8,128,128]{3,1,2,0:T(8,128)(2,1)S(1)} fusion(f32[8]{0:T(128)S(1)} %add_multiply_fusion, f32[16384]{0:T(1024)S(1)} %subtract_bitcast_fusion, s32[16]{0:T(128)S(1)} %select_reduce_fusion), kind=kOutput, calls=%fused_computation.74 | convolution fusion | flops 9830528 | bytes 589920 | tf_op jit(solution)/shard_map/dot_general | solution.py:90
  59.2 23.4 %all-to-all-done.1 = bf16[8,2,2,128,128]{4,1,3,2,0:T(2,128)(2,1)S(1)} async-done(((bf16[8,2,2,128,128]{4,1,3,2,0:T(2,128)(2,1)}), bf16[8,2,2,128,128]{4,1,3,2,0:T(2,128)(2,1)S(1)}, u32[]{:S(2)}, u32[]{:S(2)}) %all-to-all-start.1) | async-done | bytes 1048608 | tf_op jit(solution)/shard_map/all_to_all | solution.py:155
  86.7 23.6 %collective-permute-done = bf16[16,2,128,128]{2,3,1,0:T(8,128)(2,1)S(1)} collective-permute-done((bf16[16,2,128,128]{2,3,1,0:T(8,128)(2,1)S(1)}, bf16[16,2,128,128]{2,3,1,0:T(8,128)(2,1)S(1)}, u32[]{:S(2)}, u32[]{:S(2)}) %collective-permute-start) | collective-permute-done | bytes 1048608 | tf_op jit(solution)/shard_map/ppermute | solution.py:18
  110.3 21.7 %collective-permute-done.1 = bf16[16,2,128,128]{2,3,1,0:T(8,128)(2,1)S(1)} collective-permute-done((bf16[16,2,128,128]{2,3,1,0:T(8,128)(2,1)S(1)}, bf16[16,2,128,128]{2,3,1,0:T(8,128)(2,1)S(1)}, u32[]{:S(2)}, u32[]{:S(2)}) %collective-permute-start.1) | collective-permute-done | bytes 1048608 | tf_op jit(solution)/shard_map/ppermute | solution.py:18
  133.2 3.4 %convolution_bitcast_fusion = f32[16,2,2,128,128]{3,4,1,0,2:T(8,128)} fusion(bf16[1,2,128,128]{3,2,1,0:T(8,128)(2,1)S(1)} %get-tuple-element.44, bf16[1,2,128,128]{3,2,1,0:T(8,128)(2,1)S(1)} %get-tuple-element.43, bf16[16,1,2,128,128]{3,4,2,0,1:T(8,128)(2,1)S(1)} %maximum_bitcast_fusion.2, bf16[16,1,2,128,128]{3,4,2,0,1:T(8,128)(2,1)S(1)} %maximum_bitcast_fusion.1), kind=kOutput, calls=%fused_computation.5 | convolution fusion | flops 1076363264 | bytes 6422528 | tf_op jit(solution)/shard_map/npeuj,cvej->npcuv/dot_general | solution.py:49
  136.7 2.5 %fusion.96 = f32[16,2,128,128]{2,3,1,0:T(8,128)S(1)} fusion(f32[16,2,2,128,128]{3,4,1,0,2:T(8,128)} %convolution_bitcast_fusion), kind=kLoop, calls=%fused_computation.151 | loop fusion | flops 1572864 | bytes 6291456 | tf_op jit(solution)/shard_map/add | solution.py:110
  139.2 3.0 %slice_bitcast_fusion.5 = (f32[16,2,1,127,128]{3,4,1,0,2:T(8,128)}, f32[16,2,1,127,128]{3,4,1,0,2:T(8,128)}, f32[16,2,127,128]{2,3,1,0:T(8,128)S(1)}, f32[16,2,127,128]{2,3,1,0:T(8,128)S(1)}) fusion(f32[16,2,128,128]{2,3,1,0:T(8,128)S(1)} %fusion.96), kind=kLoop, calls=%fused_computation.281 | loop fusion | bytes 12484608 | tf_op jit(solution)/shard_map/jit(_roll_static)/concatenate | solution.py:114
  143.6 3.2 %slice_maximum_fusion.3 = (f32[16,2,128,127]{2,3,1,0:T(8,128)}, f32[16,2,128,127]{2,3,1,0:T(8,128)}) fusion(f32[16,2,1,128]{2,3,1,0:T(8,128)S(1)} %get-tuple-element.25, f32[16,2,127,128]{2,3,1,0:T(8,128)S(1)} %get-tuple-element.24), kind=kLoop, calls=%fused_computation.10 | loop fusion | flops 1040384 | bytes 6258688 | tf_op jit(solution)/shard_map/jit(_roll_static)/concatenate | solution.py:114
  146.9 3.3 %slice_maximum_fusion.1 = (f32[16,2,128,127]{2,3,1,0:T(8,128)}, f32[16,2,128,127]{2,3,1,0:T(8,128)}) fusion(f32[16,2,127,128]{2,3,1,0:T(8,128)S(1)} %get-tuple-element.23, f32[16,2,1,128]{2,3,1,0:T(8,128)S(1)} %get-tuple-element.26), kind=kLoop, calls=%fused_computation.8 | loop fusion | flops 1040384 | bytes 6258688 | tf_op jit(solution)/shard_map/jit(_roll_static)/concatenate | solution.py:114
  150.2 4.0 %fusion.189 = (f32[16,2,128,127]{2,3,1,0:T(8,128)}, f32[16,2,1,128,127]{3,4,1,0,2:T(8,128)}, f32[16,2,1,128,127]{3,4,1,0,2:T(8,128)}, f32[16,2,128,127]{2,3,1,0:T(8,128)}) fusion(f32[16,2,128,128]{2,3,1,0:T(8,128)S(1)} %fusion.96), kind=kLoop, calls=%fused_computation.282 | loop fusion | bytes 12484608 | tf_op jit(solution)/shard_map/jit(_roll_static)/slice | solution.py:114
  154.3 2.2 %copy.99 = f32[16,2,1,128]{3,0,2,1:T(8,128)S(1)} copy(f32[16,2,1,128]{2,3,1,0:T(8,128)} %copy-done) | data formatting | bytes 32768 | tf_op jit(solution)/shard_map/jit(_roll_static)/slice | solution.py:114
  157.1 9.2 %fusion.23 = f32[16,2]{1,0:T(8,128)S(1)} fusion(f32[16,2,128,127]{2,3,1,0:T(8,128)} %get-tuple-element.10, f32[16,2,128,1]{2,3,1,0:T(1,128)S(1)} %get-tuple-element.12, f32[16,2,128,1]{2,3,1,0:T(1,128)S(1)} %get-tuple-element.11, f32[16,2,128,127]{2,3,1,0:T(8,128)} %get-tuple-element.9, f32[16,2,128,127]{2,3,1,0:T(8,128)} %get-tuple-element.16, ...), kind=kLoop, calls=%fused_computation.39 | loop fusion | flops 11010016 | bytes 20971648 | tf_op jit(solution)/shard_map/reduce_sum | solution.py:116
  168.2 2.0 %copy.89 = f32[16,2,1,1,128]{3,4,1,0,2:T(8,128)} copy(f32[16,2,1,1,128]{4,0,3,2,1:T(8,128)S(1)} %bitcast.292) | data formatting | bytes 32768 | tf_op jit(solution)/shard_map/jit(_roll_static)/concatenate | solution.py:114
  170.3 10.6 %sqrt_bitcast_fusion = f32[16,2,128,128]{2,3,1,0:T(8,128)} fusion(f32[16,2,1,128,127]{3,4,1,0,2:T(8,128)} %bitcast.277, f32[16,2,1,128,1]{3,4,1,0,2:T(1,128)S(1)} %bitcast.289, f32[16,2,1,127,128]{3,4,1,0,2:T(8,128)} %get-tuple-element.22, f32[16,2,1,1,128]{3,4,1,0,2:T(8,128)} %copy.100, f32[16,2,1,128,1]{3,4,1,0,2:T(1,128)S(1)} %bitcast.288, ...), kind=kLoop, calls=%fused_computation.38 | loop fusion | flops 11010048 | bytes 23068800 | tf_op jit(solution)/shard_map/mul | solution.py:118
  180.8 4.3 %fusion.24 = bf16[1,16,2,2,128,128]{4,5,2,1,3,0:T(8,128)(2,1)S(1)} fusion(bf16[1,2,128,128]{3,2,1,0:T(8,128)(2,1)S(1)} %get-tuple-element.45, bf16[1,2,128,128]{3,2,1,0:T(8,128)(2,1)S(1)} %get-tuple-element.46, f32[16,2,2,128,128]{3,4,1,0,2:T(8,128)} %convolution_bitcast_fusion, f32[16,2,128,128]{2,3,1,0:T(8,128)} %sqrt_bitcast_fusion), kind=kOutput, calls=%fused_computation.54 | convolution fusion | flops 1078460416 | bytes 8519680 | tf_op jit(solution)/shard_map/npeuj,cvej->npcuv/dot_general | solution.py:49
  185.2 2.6 %copy.106 = bf16[1,16,2,2,128,128]{5,4,3,2,1,0:T(8,128)(2,1)} copy(bf16[1,16,2,2,128,128]{4,5,2,1,3,0:T(8,128)(2,1)S(1)} %fusion.24) | data formatting | bytes 4194304 | tf_op jit(solution)/shard_map/broadcast_in_dim | solution.py:171
  (63 shorter events, 15.1 us)
Async XLA Ops:
  0.0 2.6 %copy-start.5 = (f32[2,8192]{1,0:T(2,128)S(1)}, f32[2,8192]{1,0:T(2,128)}, u32[]{:S(2)}) copy-start(f32[2,8192]{1,0:T(2,128)} %param.7) | copy-start | bytes 196612
  9.3 11.4 %copy-start.6 = (s32[1,64]{1,0:T(1,128)S(1)}, s32[1,64]{1,0:T(1,128)}, u32[]{:S(2)}) copy-start(s32[1,64]{1,0:T(1,128)} %param.9) | copy-start | bytes 772
  15.8 20.2 %all-to-all-start = ((bf16[8,2,16384]{2,1,0:T(2,128)(2,1)}), bf16[8,2,16384]{2,1,0:T(2,128)(2,1)S(1)}, u32[]{:S(2)}, u32[]{:S(2)}) async-start(bf16[8,2,16384]{2,1,0:T(2,128)(2,1)} %reshape.594), calls=%async_computation | async-start | bytes 1048576 | tf_op jit(solution)/shard_map/all_to_all | solution.py:129
  40.1 9.3 %copy-start.4 = (bf16[2,128,1024]{2,1,0:T(8,128)(2,1)S(1)}, bf16[2,128,1024]{2,1,0:T(8,128)(2,1)}, u32[]{:S(2)}) copy-start(bf16[2,128,1024]{2,1,0:T(8,128)(2,1)} %param.8) | copy-start | bytes 1572868
  50.5 5.6 %copy-start.7 = (s32[1,64]{1,0:T(1,128)S(1)}, s32[1,64]{1,0:T(1,128)}, u32[]{:S(2)}) copy-start(s32[1,64]{1,0:T(1,128)} %param.10) | copy-start | bytes 772
  50.5 5.6 %copy-start.8 = (s32[1,64]{1,0:T(1,128)S(1)}, s32[1,64]{1,0:T(1,128)}, u32[]{:S(2)}) copy-start(s32[1,64]{1,0:T(1,128)} %param.11) | copy-start | bytes 772
  52.5 30.1 %all-to-all-start.1 = ((bf16[8,2,2,128,128]{4,1,3,2,0:T(2,128)(2,1)}), bf16[8,2,2,128,128]{4,1,3,2,0:T(2,128)(2,1)S(1)}, u32[]{:S(2)}, u32[]{:S(2)}) async-start(bf16[8,2,2,128,128]{4,1,3,2,0:T(2,128)(2,1)} %copy.79), calls=%async_computation.1 | async-start | bytes 2097152 | tf_op jit(solution)/shard_map/all_to_all | solution.py:155
  84.4 25.8 %collective-permute-start = (bf16[16,2,128,128]{2,3,1,0:T(8,128)(2,1)S(1)}, bf16[16,2,128,128]{2,3,1,0:T(8,128)(2,1)S(1)}, u32[]{:S(2)}, u32[]{:S(2)}) collective-permute-start(bf16[16,2,128,128]{2,3,1,0:T(8,128)(2,1)S(1)} %fusion.35), channel_id=1, source_target_pairs={{0,24},{8,0},{16,8},{24,16},{1,25},{9,1},{17,9},{25,17},{2,26},{10... | collective-permute-start | bytes 3145736 | tf_op jit(solution)/shard_map/ppermute | solution.py:18
  85.2 46.8 %collective-permute-start.1 = (bf16[16,2,128,128]{2,3,1,0:T(8,128)(2,1)S(1)}, bf16[16,2,128,128]{2,3,1,0:T(8,128)(2,1)S(1)}, u32[]{:S(2)}, u32[]{:S(2)}) collective-permute-start(bf16[16,2,128,128]{2,3,1,0:T(8,128)(2,1)S(1)} %fusion.35), channel_id=1, source_target_pairs={{0,16},{8,24},{16,0},{24,8},{1,17},{9,25},{17,1},{25,9},{2,18},{10... | collective-permute-start | bytes 3145736 | tf_op jit(solution)/shard_map/ppermute | solution.py:18
  142.2 1.4 copy-start.2
  142.2 4.7 %copy-start.1 = (f32[16,2,127,128]{2,3,1,0:T(8,128)}, f32[16,2,127,128]{2,3,1,0:T(8,128)S(1)}, u32[]{:S(2)}) copy-start(f32[16,2,127,128]{2,3,1,0:T(8,128)S(1)} %get-tuple-element.23) | copy-start | bytes 6242308
  143.0 4.0 %copy-start = (f32[16,2,1,128]{2,3,1,0:T(8,128)}, f32[16,2,1,128]{2,3,1,0:T(8,128)S(1)}, u32[]{:S(2)}) copy-start(f32[16,2,1,128]{2,3,1,0:T(8,128)S(1)} %get-tuple-element.26) | copy-start | bytes 49156
  166.3 4.0 %copy-start.3 = (f32[16,2,128,127]{2,3,1,0:T(8,128)S(1)}, f32[16,2,128,127]{2,3,1,0:T(8,128)}, u32[]{:S(2)}) copy-start(f32[16,2,128,127]{2,3,1,0:T(8,128)} %get-tuple-element.5) | copy-start | bytes 6242308
where the time goes:
time: 188 us
  waiting for transfers between devices  83.7 us (45%)
  local copies, waits for them, and re-layouts  46 us (24%)
  other arithmetic  33.5 us (18%)
  matrix products  13.5 us (7%)
  starting transfers between devices  10.7 us (6%)
    ppermute x2, waiting for transfers between devices, passed_along(): return lax.ppermute(value, axis, pairs)  45.3 us
    all_to_all x1, waiting for transfers between devices, body(): lax.all_to_all(outbox, 'shard', split_axis=0, concat_axis=0, tiled=True)  23.4 us
    all_to_all x1, waiting for transfers between devices, body(): lax.all_to_all(compressed, 'shard', split_axis=2, concat_axis=1, tiled=True)  15 us
    unnamed x24, local copies, waits for them, and re-layouts  11.4 us
    dot_general x9, matrix products, bdot(): return jnp.einsum(form, left, right, preferred_element_type=jnp.float32)  10.7 us
    mul x1, other arithmetic, goldstein(): weighted = (spectrum * weight[:, :, None]).astype(jnp.bfloat16)  10.6 us
    reduce_sum x1, other arithmetic, goldstein(): level = jnp.mean(smooth, axis=(-2, -1), keepdims=True)  9.16 us
    all_to_all x1, local copies, waits for them, and re-layouts, body(): lax.all_to_all(compressed, 'shard', split_axis=2, concat_axis=1, tiled=True)  8.96 us
  transfers between devices with their start and end apart: 4, of which 4 were waited for; matrix products, arithmetic and copies ran while one was open for 2% of the time, Pallas kernels for 0%

commit v1 on v0

v1 whole, which is shorter than its diff:
```python
import functools
import math

import jax
import jax.numpy as jnp
import ml_dtypes
import numpy as np
from jax import lax
from jax.experimental import pallas as pl
from jax.experimental.pallas import tpu as pltpu
from jax.sharding import PartitionSpec as P

BLK = 128
NSUB = 8
BLK_DEV = 8
BF = jnp.bfloat16
F32 = jnp.float32


def dft_parts(size, sign):
    index = np.arange(size)
    angle = 2.0 * math.pi / size * (index[:, None] * index[None, :] % size)
    scale = 1.0 / math.sqrt(size)
    return np.cos(angle) * scale, sign * np.sin(angle) * scale


def left_table(size, sign):
    cosine, sine = dft_parts(size, sign)
    return np.block([[cosine, -sine], [sine, cosine]]).astype(ml_dtypes.bfloat16)


def right_table(size, sign):
    return np.ascontiguousarray(left_table(size, sign).T)


def first_table(rng):
    outer, inner = BLK, rng // BLK
    low = outer * BLK // rng
    cosine, sine = dft_parts(outer, 1)
    full = np.stack([np.stack([cosine, sine], 1), np.stack([-sine, cosine], 1)])
    full = full.reshape(2, outer // low, low, 2 * outer)
    return np.transpose(full, (2, 0, 1, 3)).reshape(2 * outer, 2 * outer).astype(ml_dtypes.bfloat16)


def twiddle_table(rng):
    inner = rng // BLK
    phase = np.arange(inner)[:, None] * np.arange(BLK)[None, :] % rng
    angle = 2.0 * math.pi / rng * phase
    return np.stack([np.cos(angle), np.sin(angle)]).astype(np.float32)


def kernel_table():
    offset = (np.arange(NSUB) + 0.5) / NSUB
    cells = np.arange(BLK)
    dist = cells[None, None, :] - cells[None, :, None] - offset[:, None, None]
    window = np.where(np.abs(dist) < 4.0, 0.5 + 0.5 * np.cos(math.pi * dist / 4.0), 0.0)
    return (np.sinc(dist) * window).astype(ml_dtypes.bfloat16)


def mm(left, right):
    return jnp.dot(left, right, preferred_element_type=F32)


def kernel(
    n,
    dates,
    most,
    capacity,
    src_ref,
    kind_ref,
    entry_ref,
    valid_ref,
    echo_ref,
    rref_ref,
    aref_ref,
    t1_ref,
    tw_ref,
    w2_ref,
    pf_ref,
    pb_ref,
    kt_ref,
    gfl_ref,
    gfr_ref,
    gbl_ref,
    gbr_ref,
    out_ref,
    lhs,
    mat,
    snd,
    cols,
    blocks,
    outbox,
    inbox,
    ybox,
    xbox,
    fil,
    s1,
    r1,
    s2,
    r2,
    sy,
    ry,
    sx,
    rx,
):
    me = lax.axis_index("shard")
    day = lax.axis_index("date")
    grp = lax.axis_index("grp")
    relay = dates == 4
    ydst = lax.rem(day + dates - 2, dates)
    if relay:
        parity = lax.rem(day, 2)
        xdst = day + 1 - 2 * parity
        xsrc = xdst
    else:
        xdst = lax.rem(day + dates - 1, dates)
        xsrc = lax.rem(day + 1, dates)
    ysrc = lax.rem(day + 2, dates)
    mesh_id = pl.DeviceIdType.MESH

    barrier = pltpu.get_barrier_semaphore()

    def greet(k, _):
        pl.semaphore_signal(
            barrier, inc=1, device_id=(grp, day, lax.rem(me + k, n)), device_id_type=mesh_id
        )
        return 0

    lax.fori_loop(1, n, greet, 0)
    for other in (ysrc, xsrc):
        pl.semaphore_signal(barrier, inc=1, device_id=(grp, other, me), device_id_type=mesh_id)

    pulses = echo_ref.shape[1]
    rng = echo_ref.shape[2]
    tiles = rng // BLK
    inner = rng // BLK
    mine = tiles // n
    wide = n * pulses

    real = echo_ref[0].astype(F32)
    imag = echo_ref[1].astype(F32)
    rre = rref_ref[0:1, :]
    rim = rref_ref[1:2, :]
    mat[0] = (real * rre + imag * rim).reshape(pulses, tiles, BLK)
    mat[1] = (imag * rre - real * rim).reshape(pulses, tiles, BLK)

    for p in range(pulses):
        both = jnp.concatenate([mat[0, p], mat[1, p]], axis=0).T
        low = BLK // inner
        parts = [both[x * inner : (x + 1) * inner] for x in range(low)]
        lhs[p * inner : (p + 1) * inner, :] = jnp.concatenate(parts, axis=1).astype(BF)

    twc = tw_ref[0]
    tws = tw_ref[1]
    group = 4
    for g in range(0, pulses, group):
        section = mm(lhs[g * inner : (g + group) * inner, :], t1_ref[...])
        rights = []
        for p in range(group):
            sre = section[p * inner : (p + 1) * inner, :BLK]
            sim = section[p * inner : (p + 1) * inner, BLK:]
            rights.append(
                jnp.concatenate([sre * twc - sim * tws, sre * tws + sim * twc], axis=0).astype(BF)
            )
        second = mm(w2_ref[...], jnp.concatenate(rights, axis=1))
        for p in range(group):
            mat[:, g + p] = second[:, p * BLK : (p + 1) * BLK].reshape(2, tiles, BLK)
    for c in range(2):
        snd[c] = jnp.swapaxes(mat[c], 0, 1).astype(BF)

    pl.semaphore_wait(barrier, n + 1)

    def copy_one(k):
        dest = lax.rem(me + k, n)
        return pltpu.make_async_remote_copy(
            src_ref=snd.at[:, pl.ds(dest * mine, mine)],
            dst_ref=cols.at[:, :, pl.ds(me * pulses, pulses)],
            send_sem=s1.at[k],
            recv_sem=r1.at[k],
            device_id=(grp, day, dest),
            device_id_type=mesh_id,
        )

    def wait_one(k):
        source = lax.rem(me + n - k, n)
        return pltpu.make_async_remote_copy(
            src_ref=snd.at[:, pl.ds(me * mine, mine)],
            dst_ref=cols.at[:, :, pl.ds(source * pulses, pulses)],
            send_sem=s1.at[k],
            recv_sem=r1.at[k],
            device_id=(grp, day, source),
            device_id_type=mesh_id,
        )

    def start_one(k, _):
        copy_one(k).start()
        return 0

    def end_one(k, _):
        wait_one(k).wait_recv()
        return 0

    lax.fori_loop(1, n, start_one, 0)
    cols[:, :, pl.ds(me * pulses, pulses)] = snd[:, pl.ds(me * mine, mine)]
    lax.fori_loop(1, n, end_one, 0)

    rows_of = wide // BLK
    for j in range(0, mine, 2):
        right = jnp.concatenate(
            [
                jnp.concatenate([cols[0, j], cols[1, j]], axis=0),
                jnp.concatenate([cols[0, j + 1], cols[1, j + 1]], axis=0),
            ],
            axis=1,
        )
        doppler = mm(pf_ref[...], right)
        are = aref_ref[0, :, j * BLK : (j + 2) * BLK].astype(F32)
        aim = aref_ref[1, :, j * BLK : (j + 2) * BLK].astype(F32)
        dre = doppler[:wide]
        dim = doppler[wide:]
        shaped = jnp.concatenate([dre * are - dim * aim, dre * aim + dim * are], axis=0).astype(BF)
        image = mm(pb_ref[...], shaped).astype(BF)
        for x in range(2):
            for y in range(rows_of):
                for c in range(2):
                    low = c * wide + y * BLK
                    blocks[y * mine + j + x, :, c * BLK : (c + 1) * BLK] = image[
                        low : low + BLK, x * BLK : (x + 1) * BLK
                    ]

    def resampled(k, r):
        at = k * most + r
        return mm(kt_ref[kind_ref[at]], blocks[src_ref[at]]).astype(BF)

    for r in range(most):
        inbox[0, r] = resampled(0, r)

    def copy_two(k, dest):
        return pltpu.make_async_remote_copy(
            src_ref=outbox.at[k],
            dst_ref=inbox.at[k],
            send_sem=s2.at[k],
            recv_sem=r2.at[k],
            device_id=(grp, day, dest),
            device_id_type=mesh_id,
        )

    def start_two(k, _):
        for r in range(most):
            outbox[k, r] = resampled(k, r)
        copy_two(k, lax.rem(me + k, n)).start()
        return 0

    lax.fori_loop(1, n, start_two, 0)

    def copy_y(k):
        return pltpu.make_async_remote_copy(
            src_ref=inbox.at[k],
            dst_ref=ybox.at[k],
            send_sem=sy.at[k],
            recv_sem=ry.at[k],
            device_id=(grp, ydst, me),
            device_id_type=mesh_id,
        )

    def copy_x(k, source):
        return pltpu.make_async_remote_copy(
            src_ref=source.at[k],
            dst_ref=xbox.at[k],
            send_sem=sx.at[k],
            recv_sem=rx.at[k],
            device_id=(grp, xdst, me),
            device_id_type=mesh_id,
        )

    def stage_a(k):
        @pl.when(k > 0)
        def _():
            copy_two(k, lax.rem(me + k, n)).wait_recv()

        copy_y(k).start()
        if relay:

            @pl.when(parity == 1)
            def _():
                copy_x(k, inbox).start()
        else:
            copy_x(k, inbox).start()

    def stage_b(k):
        copy_y(k).wait_recv()
        if relay:

            @pl.when(parity == 0)
            def _():
                copy_x(k, ybox).start()

    def patches(k, r):
        own = inbox[k, r].astype(F32)
        ore = own[:, :BLK]
        oim = own[:, BLK:]
        tops = []
        lows = []
        for box in (xbox, ybox):
            oth = box[k, r].astype(F32)
            tre = oth[:, :BLK]
            tim = oth[:, BLK:]
            tops.append(ore * tre + oim * tim)
            lows.append(oim * tre - ore * tim)
        pair = jnp.concatenate(
            [jnp.concatenate(tops, axis=1), jnp.concatenate(lows, axis=1)], axis=0
        ).astype(BF)

        def turned(x):
            return jnp.concatenate(
                [
                    jnp.concatenate([x[:BLK, :BLK], x[BLK:, :BLK]], axis=1),
                    jnp.concatenate([x[:BLK, BLK:], x[BLK:, BLK:]], axis=1),
                ],
                axis=0,
            )

        rows = mm(gfl_ref[...], pair).astype(BF)
        spectrum = mm(turned(rows), gfr_ref[...])
        weighted = []
        for x in range(2):
            spec = spectrum[x * BLK : (x + 1) * BLK]
            sre = spec[:, :BLK]
            sim = spec[:, BLK:]
            power = sre * sre + sim * sim
            line = power + pltpu.roll(power, 1, 1) + pltpu.roll(power, BLK - 1, 1)
            smooth = (line + pltpu.roll(line, 1, 0) + pltpu.roll(line, BLK - 1, 0)) * (1.0 / 9.0)
            level = jnp.sum(jnp.sum(smooth, axis=0, keepdims=True), axis=1, keepdims=True)
            level = level * (1.0 / (BLK * BLK)) + 1e-06
            weight = lax.rsqrt(lax.rsqrt(smooth * (1.0 / level)))
            weighted.append(jnp.concatenate([sre * weight, sim * weight], axis=1))
        weighted = jnp.concatenate(weighted, axis=0).astype(BF)
        back = mm(gbl_ref[...], turned(weighted)).astype(BF)
        done = mm(turned(back), gbr_ref[...]).astype(BF)
        at = k * most + r
        for x in range(2):
            for c in range(2):
                fil[at, x, c] = done[x * BLK : (x + 1) * BLK, c * BLK : (c + 1) * BLK]

    def stage_c(k):
        copy_x(k, inbox).wait_recv()
        for r in range(most):
            patches(k, r)

    stage_a(0)
    stage_a(1)
    stage_b(0)

    def step(k, _):
        stage_a(k)
        stage_b(k - 1)
        stage_c(k - 2)
        return 0

    lax.fori_loop(2, n, step, 0)
    stage_b(n - 1)

    def last(k, _):
        stage_c(k)
        return 0

    lax.fori_loop(n - 2, n, last, 0)

    def place(q, _):
        found = fil[entry_ref[q]]
        out_ref[q] = jnp.where(valid_ref[q] == 1, found, jnp.zeros_like(found))
        return 0

    lax.fori_loop(0, capacity, place, 0)

    def drain(k, _):
        @pl.when(k > 0)
        def _():
            copy_one(k).wait_send()
            copy_two(k, lax.rem(me + k, n)).wait_send()

        copy_y(k).wait_send()
        copy_x(k, inbox).wait_send()
        return 0

    lax.fori_loop(0, n, drain, 0)


def body(dates, echo_spectra, range_reference, azimuth_reference, block_owner, block_slot, kernel_index):
    n = lax.axis_size("shard")
    most = max(2, 2 * BLK_DEV // n)
    capacity = min(2 * BLK_DEV, n * most)
    me = lax.axis_index("shard")
    owners = block_owner[0].reshape(n, BLK_DEV)
    slots = block_slot[0]
    local = jnp.arange(BLK_DEV, dtype=jnp.int32)
    earlier = (owners[:, :, None] == owners[:, None, :]) & (local[None, None, :] < local[None, :, None])
    rank = jnp.sum(earlier.astype(jnp.int32), axis=2)
    steps = jnp.arange(n, dtype=jnp.int32)
    my_owner = lax.dynamic_index_in_dim(owners, me, 0, keepdims=False)
    my_rank = lax.dynamic_index_in_dim(rank, me, 0, keepdims=False)
    my_kind = lax.dynamic_index_in_dim(kernel_index[0].reshape(n, BLK_DEV), me, 0, keepdims=False)
    my_place = (my_owner - me + n) % n * most + my_rank
    match = (my_place[None, :] == jnp.arange(n * most, dtype=jnp.int32)[:, None]).astype(jnp.int32)
    source = jnp.sum(match * local[None, :], axis=1)
    kind = jnp.sum(match * my_kind[None, :], axis=1)
    entry_of = ((me - steps + n) % n * most)[:, None] + rank
    hit = (slots[None, :] == jnp.arange(capacity, dtype=jnp.int32)[:, None]) & (
        owners.reshape(-1) == me
    )[None, :]
    entry = jnp.sum(hit.astype(jnp.int32) * entry_of.reshape(-1)[None, :], axis=1)
    valid = jnp.max(hit.astype(jnp.int32), axis=1)

    echo = echo_spectra[0]
    pulses, rng = echo.shape[1:]
    inner = rng // BLK
    mine = rng // BLK // n
    wide = pulses * n
    tables = [
        first_table(rng),
        twiddle_table(rng),
        left_table(inner, 1),
        left_table(wide, -1),
        left_table(wide, 1),
        kernel_table(),
        left_table(BLK, -1),
        right_table(BLK, -1),
        left_table(BLK, 1),
        right_table(BLK, 1),
    ]
    smem = pl.BlockSpec(memory_space=pltpu.SMEM)
    vmem = pl.BlockSpec(memory_space=pltpu.VMEM)
    box = pltpu.VMEM((n, most, BLK, 2 * BLK), BF)
    sems = pltpu.SemaphoreType.DMA((n,))
    out = pl.pallas_call(
        functools.partial(kernel, n, dates, most, capacity),
        out_shape=jax.ShapeDtypeStruct((capacity, 2, 2, BLK, BLK), BF),
        in_specs=[smem] * 4 + [vmem] * 13,
        out_specs=vmem,
        scratch_shapes=[
            pltpu.VMEM((pulses * inner, 2 * BLK), BF),
            pltpu.VMEM((2, pulses, rng // BLK, BLK), F32),
            pltpu.VMEM((2, rng // BLK, pulses, BLK), BF),
            pltpu.VMEM((2, mine, wide, BLK), BF),
            pltpu.VMEM((BLK_DEV, BLK, 2 * BLK), BF),
            box,
            box,
            box,
            box,
            pltpu.VMEM((n * most, 2, 2, BLK, BLK), BF),
            *[sems] * 8,
        ],
        compiler_params=pltpu.CompilerParams(collective_id=0, has_side_effects=True),
    )(source, kind, entry, valid, echo, range_reference, azimuth_reference, *[jnp.asarray(t) for t in tables])
    return out[None]


def solution(mesh):
    in_specs = (
        P(("grp", "date"), None, "shard", None),
        P(),
        P(None, None, "shard"),
        P(("grp", "date"), None),
        P(("grp", "date"), None),
        P(("grp", "date"), None),
    )
    out_specs = P(("grp", "date"), "shard", None, None, None, None)
    return jax.shard_map(
        functools.partial(body, mesh.shape["date"]),
        mesh=mesh,
        in_specs=in_specs,
        out_specs=out_specs,
        check_vma=False,
    )
```

time: 188 us -> 72.9 us (0.39)
  the two profiles are of different devices: /device:TPU:2 before, /device:TPU:26 now
where the time goes in v1:
time: 72.9 us; the launch traced here: 72.7 us
  Pallas kernels  63.2 us (87%)
  other arithmetic  5.63 us (8%)
  local copies, waits for them, and re-layouts  3.91 us (5%)
    pallas_call x1, Pallas kernels, body(): pl.pallas_call(functools.partial(kernel, n, dates, most, capacity), out_s...  63.2 us
    unnamed x2, local copies, waits for them, and re-layouts  3.67 us
    unnamed x2, other arithmetic  2.64 us

profile of v1, /device:TPU:26, one launch (start us, length us, event | category | flops | bytes accessed | tf_op | source)
XLA Modules:
  0.0 72.7 jit_solution(3617187895132786067)
XLA Ops:
  0.0 0.5 broadcast.101
  0.5 1.3 %reduce.7 = s32[64]{0:T(128)S(1)} reduce(s32[1,64]{1,0:T(1,128)} %param.21, s32[]{:T(128)} %broadcast.101), dimensions={0}, to_apply=%param.21.reduce_sub_computation.3 | reduce | bytes 516 | tf_op args[5]
  1.8 1.3 %reduce.6 = s32[64]{0:T(128)S(1)} reduce(s32[1,64]{1,0:T(1,128)} %param.19, s32[]{:T(128)} %broadcast.101), dimensions={0}, to_apply=%param.19.reduce_sub_computation.3 | reduce | bytes 516 | tf_op args[3]
  3.1 0.7 compare_bitcast_fusion
  3.8 0.1 reshape_squeeze.6
  3.9 0.3 convert_reduce_fusion
  4.2 0.1 broadcast_add_fusion
  4.3 0.1 add.59
  4.4 1.3 %convert_reduce_fusion.1 = (s32[16]{0:T(128)}, s32[16]{0:T(128)}) fusion(s32[64]{0:T(128)} %bitcast.11, pred[64]{0:T(512)(128)(4,1)S(1)} %compare_bitcast_fusion, s32[64]{0:T(128)S(1)} %add.59), kind=kLoop, calls=%fused_computation.1 | loop fusion | flops 6112 | bytes 704 | tf_op jit(solution)/shard_map/reduce_max | solution.py:412
  5.7 0.1 reshape_squeeze.7
  5.8 0.6 select_reduce_fusion.1
  6.4 63.2 %shard_map.154 = bf16[16,2,2,128,128]{4,3,2,1,0:T(8,128)(2,1)} custom-call(s32[16]{0:T(128)} %get-tuple-element.8.src_ref, s32[16]{0:T(128)} %get-tuple-element.7.kind_ref, s32[16]{0:T(128)} %get-tuple-element.6.entry_ref, s32[16]{0:T(128)} %get-tuple-element.5.valid_ref, bf16[2,16,8192]{2,1,0:T(8,128)(2,1)} %bitcast.10, f32[2,8192]{1,0:T(2,128)} %rref_ref.1, ...), custom_call_target="tpu_custom_call" | custom-call | tf_op jit(solution)/shard_map/pallas_call | solution.py:435
  69.6 3.2 %copy.18 = bf16[1,16,2,2,128,128]{5,4,3,2,1,0:T(8,128)(2,1)} copy(bf16[1,16,2,2,128,128]{5,4,3,2,1,0:T(8,128)(2,1)} %bitcast.9) | data formatting | bytes 4194304
  (3 shorter events, 0.0 us)

commit v2 on v1

--- a/solution.py
+++ b/solution.py
@@ -66,10 +66,9 @@
     dates,
     most,
     capacity,
-    src_ref,
-    kind_ref,
-    entry_ref,
-    valid_ref,
+    owner_ref,
+    slot_ref,
+    kinds_ref,
     echo_ref,
     rref_ref,
     aref_ref,
@@ -83,7 +82,10 @@
     gfr_ref,
     gbl_ref,
     gbr_ref,
-    out_ref,
+    fil,
+    entry_ref,
+    src_ref,
+    kind_ref,
     lhs,
     mat,
     snd,
@@ -93,7 +95,6 @@
     inbox,
     ybox,
     xbox,
-    fil,
     s1,
     r1,
     s2,
@@ -202,6 +203,38 @@
 
     lax.fori_loop(1, n, start_one, 0)
     cols[:, :, pl.ds(me * pulses, pulses)] = snd[:, pl.ds(me * mine, mine)]
+
+    def sources(k, _):
+        dest = lax.rem(me + k, n)
+        seen = jnp.int32(0)
+        found = [jnp.int32(0)] * most
+        for b in range(BLK_DEV):
+            named = owner_ref[0, me * BLK_DEV + b] == dest
+            for r in range(most):
+                found[r] = jnp.where(named & (seen == r), b, found[r])
+            seen = seen + named.astype(jnp.int32)
+        for r in range(most):
+            src_ref[k * most + r] = found[r]
+            kind_ref[k * most + r] = kinds_ref[0, me * BLK_DEV + found[r]]
+        return 0
+
+    lax.fori_loop(0, n, sources, 0)
+
+    def entries(t, held):
+        held = list(held)
+        at = lax.rem(me - t + n, n) * most
+        for b in range(BLK_DEV):
+            named = owner_ref[0, t * BLK_DEV + b] == me
+            slot = jnp.where(named, slot_ref[0, t * BLK_DEV + b], -1)
+            for q in range(capacity):
+                held[q] = jnp.where(slot == q, at, held[q])
+            at = at + named.astype(jnp.int32)
+        return tuple(held)
+
+    held = lax.fori_loop(0, n, entries, (jnp.int32(n * most),) * capacity)
+    for q in range(capacity):
+        entry_ref[q] = held[q]
+    fil[n * most] = jnp.zeros_like(fil[n * most])
     lax.fori_loop(1, n, end_one, 0)
 
     rows_of = wide // BLK
@@ -366,13 +399,6 @@
 
     lax.fori_loop(n - 2, n, last, 0)
 
-    def place(q, _):
-        found = fil[entry_ref[q]]
-        out_ref[q] = jnp.where(valid_ref[q] == 1, found, jnp.zeros_like(found))
-        return 0
-
-    lax.fori_loop(0, capacity, place, 0)
-
     def drain(k, _):
         @pl.when(k > 0)
         def _():
@@ -386,31 +412,20 @@
     lax.fori_loop(0, n, drain, 0)
 
 
+def place(capacity, entry_ref, fil, out_ref, sems):
+    def copy(q):
+        return pltpu.make_async_copy(fil.at[entry_ref[q]], out_ref.at[q], sems.at[q])
+
+    for q in range(capacity):
+        copy(q).start()
+    for q in range(capacity):
+        copy(q).wait()
+
+
 def body(dates, echo_spectra, range_reference, azimuth_reference, block_owner, block_slot, kernel_index):
     n = lax.axis_size("shard")
     most = max(2, 2 * BLK_DEV // n)
     capacity = min(2 * BLK_DEV, n * most)
-    me = lax.axis_index("shard")
-    owners = block_owner[0].reshape(n, BLK_DEV)
-    slots = block_slot[0]
-    local = jnp.arange(BLK_DEV, dtype=jnp.int32)
-    earlier = (owners[:, :, None] == owners[:, None, :]) & (local[None, None, :] < local[None, :, None])
-    rank = jnp.sum(earlier.astype(jnp.int32), axis=2)
-    steps = jnp.arange(n, dtype=jnp.int32)
-    my_owner = lax.dynamic_index_in_dim(owners, me, 0, keepdims=False)
-    my_rank = lax.dynamic_index_in_dim(rank, me, 0, keepdims=False)
-    my_kind = lax.dynamic_index_in_dim(kernel_index[0].reshape(n, BLK_DEV), me, 0, keepdims=False)
-    my_place = (my_owner - me + n) % n * most + my_rank
-    match = (my_place[None, :] == jnp.arange(n * most, dtype=jnp.int32)[:, None]).astype(jnp.int32)
-    source = jnp.sum(match * local[None, :], axis=1)
-    kind = jnp.sum(match * my_kind[None, :], axis=1)
-    entry_of = ((me - steps + n) % n * most)[:, None] + rank
-    hit = (slots[None, :] == jnp.arange(capacity, dtype=jnp.int32)[:, None]) & (
-        owners.reshape(-1) == me
-    )[None, :]
-    entry = jnp.sum(hit.astype(jnp.int32) * entry_of.reshape(-1)[None, :], axis=1)
-    valid = jnp.max(hit.astype(jnp.int32), axis=1)
-
     echo = echo_spectra[0]
     pulses, rng = echo.shape[1:]
     inner = rng // BLK
@@ -432,12 +447,17 @@
     vmem = pl.BlockSpec(memory_space=pltpu.VMEM)
     box = pltpu.VMEM((n, most, BLK, 2 * BLK), BF)
     sems = pltpu.SemaphoreType.DMA((n,))
-    out = pl.pallas_call(
+    filtered, entry = pl.pallas_call(
         functools.partial(kernel, n, dates, most, capacity),
-        out_shape=jax.ShapeDtypeStruct((capacity, 2, 2, BLK, BLK), BF),
-        in_specs=[smem] * 4 + [vmem] * 13,
-        out_specs=vmem,
+        out_shape=(
+            jax.ShapeDtypeStruct((n * most + 1, 2, 2, BLK, BLK), BF),
+            jax.ShapeDtypeStruct((capacity,), jnp.int32),
+        ),
+        in_specs=[smem] * 3 + [vmem] * 13,
+        out_specs=(vmem, smem),
         scratch_shapes=[
+            pltpu.SMEM((n * most,), jnp.int32),
+            pltpu.SMEM((n * most,), jnp.int32),
             pltpu.VMEM((pulses * inner, 2 * BLK), BF),
             pltpu.VMEM((2, pulses, rng // BLK, BLK), F32),
             pltpu.VMEM((2, rng // BLK, pulses, BLK), BF),
@@ -447,11 +467,25 @@
             box,
             box,
             box,
-            pltpu.VMEM((n * most, 2, 2, BLK, BLK), BF),
             *[sems] * 8,
         ],
         compiler_params=pltpu.CompilerParams(collective_id=0, has_side_effects=True),
-    )(source, kind, entry, valid, echo, range_reference, azimuth_reference, *[jnp.asarray(t) for t in tables])
+    )(
+        block_owner,
+        block_slot,
+        kernel_index,
+        echo,
+        range_reference,
+        azimuth_reference,
+        *[jnp.asarray(t) for t in tables],
+    )
+    out = pl.pallas_call(
+        functools.partial(place, capacity),
+        out_shape=jax.ShapeDtypeStruct((capacity, 2, 2, BLK, BLK), BF),
+        in_specs=[smem, vmem],
+        out_specs=pl.BlockSpec(memory_space=pl.ANY),
+        scratch_shapes=[pltpu.SemaphoreType.DMA((capacity,))],
+    )(entry, filtered)
     return out[None]
 
 

time: 72.9 us -> 65.9 us (0.904)
  other arithmetic: 5.63 us -> 0 us
  local copies, waits for them, and re-layouts: 3.91 us -> 0 us
  Pallas kernels: 63.2 us -> 65.7 us
    unnamed x2 -> x0, local copies, waits for them, and re-layouts: 3.67 us -> none
    pallas_call x0 -> x1, Pallas kernels: none -> 3.08 us  [body(): pl.pallas_call(functools.partial(place, capacity), out_shape=jax.ShapeDty...]
    unnamed x2 -> x0, other arithmetic: 2.64 us -> none
    reduce_max x1 -> x0, other arithmetic: 1.32 us -> none  [body(): valid = jnp.max(hit.astype(jnp.int32), axis=1)]
    reduce_sum x2 -> x0, other arithmetic: 0.9 us -> none  [the longest x1 0.61 us: body(): kind = jnp.sum(match * my_kind[None, :], axis=1)]
where the time goes in v2:
time: 65.9 us; the launch traced here: 65.7 us
  Pallas kernels  65.7 us (100%)
    pallas_call x1, Pallas kernels, body(): pl.pallas_call(functools.partial(kernel, n, dates, most, capacity), out_s...  62.7 us
    pallas_call x1, Pallas kernels, body(): pl.pallas_call(functools.partial(place, capacity), out_shape=jax.ShapeDty...  3.08 us

profile of v2, /device:TPU:26, one launch (start us, length us, event | category | flops | bytes accessed | tf_op | source)
XLA Modules:
  0.0 65.7 jit_solution(3414548078991114946)
XLA Ops:
  0.0 62.7 %shard_map.154 = (bf16[17,2,2,128,128]{4,3,2,1,0:T(8,128)(2,1)}, s32[16]{0:T(128)}) custom-call(s32[1,64]{1,0:T(1,128)} %owner_ref.1, s32[1,64]{1,0:T(1,128)} %slot_ref.1, s32[1,64]{1,0:T(1,128)} %kinds_ref.1, bf16[2,16,8192]{2,1,0:T(8,128)(2,1)} %bitcast.2, f32[2,8192]{1,0:T(2,128)} %rref_ref.1, bf16[2,128,1024]{2,1,0:T(8,128)(2,1)} %aref_ref.1, ...), custom_call_target="tpu_custom_call" | custom-call | tf_op jit(solution)/shard_map/pallas_call | solution.py:450
  62.7 3.1 %shard_map.155 = bf16[16,2,2,128,128]{4,3,2,1,0:T(8,128)(2,1)} custom-call(s32[16]{0:T(128)} %get-tuple-element.7.entry_ref, bf16[17,2,2,128,128]{4,3,2,1,0:T(8,128)(2,1)} %get-tuple-element.8.fil), custom_call_target="tpu_custom_call" | custom-call | tf_op jit(solution)/shard_map/pallas_call | solution.py:482

commit v3 on v2

--- a/solution.py
+++ b/solution.py
@@ -55,6 +55,15 @@
     dist = cells[None, None, :] - cells[None, :, None] - offset[:, None, None]
     window = np.where(np.abs(dist) < 4.0, 0.5 + 0.5 * np.cos(math.pi * dist / 4.0), 0.0)
     return (np.sinc(dist) * window).astype(ml_dtypes.bfloat16)
+
+
+def flipped(a, b, n):
+    total = 0
+    bit = 1
+    while bit < n:
+        total = total + (a // bit + b // bit) % 2 * bit
+        bit *= 2
+    return total
 
 
 def mm(left, right):
@@ -123,7 +132,7 @@
 
     def greet(k, _):
         pl.semaphore_signal(
-            barrier, inc=1, device_id=(grp, day, lax.rem(me + k, n)), device_id_type=mesh_id
+            barrier, inc=1, device_id=(grp, day, flipped(me, k, n)), device_id_type=mesh_id
         )
         return 0
 
@@ -172,7 +181,7 @@
     pl.semaphore_wait(barrier, n + 1)
 
     def copy_one(k):
-        dest = lax.rem(me + k, n)
+        dest = flipped(me, k, n)
         return pltpu.make_async_remote_copy(
             src_ref=snd.at[:, pl.ds(dest * mine, mine)],
             dst_ref=cols.at[:, :, pl.ds(me * pulses, pulses)],
@@ -183,7 +192,7 @@
         )
 
     def wait_one(k):
-        source = lax.rem(me + n - k, n)
+        source = flipped(me, k, n)
         return pltpu.make_async_remote_copy(
             src_ref=snd.at[:, pl.ds(me * mine, mine)],
             dst_ref=cols.at[:, :, pl.ds(source * pulses, pulses)],
@@ -205,7 +214,7 @@
     cols[:, :, pl.ds(me * pulses, pulses)] = snd[:, pl.ds(me * mine, mine)]
 
     def sources(k, _):
-        dest = lax.rem(me + k, n)
+        dest = flipped(me, k, n)
         seen = jnp.int32(0)
         found = [jnp.int32(0)] * most
         for b in range(BLK_DEV):
@@ -222,7 +231,7 @@
 
     def entries(t, held):
         held = list(held)
-        at = lax.rem(me - t + n, n) * most
+        at = flipped(me, t, n) * most
         for b in range(BLK_DEV):
             named = owner_ref[0, t * BLK_DEV + b] == me
             slot = jnp.where(named, slot_ref[0, t * BLK_DEV + b], -1)
@@ -261,30 +270,29 @@
                         low : low + BLK, x * BLK : (x + 1) * BLK
                     ]
 
-    def resampled(k, r):
-        at = k * most + r
+    def resampled(at):
         return mm(kt_ref[kind_ref[at]], blocks[src_ref[at]]).astype(BF)
 
-    for r in range(most):
-        inbox[0, r] = resampled(0, r)
-
-    def copy_two(k, dest):
+    total = n * most
+    for e in range(most):
+        inbox[e] = resampled(e)
+
+    def copy_two(e):
         return pltpu.make_async_remote_copy(
-            src_ref=outbox.at[k],
-            dst_ref=inbox.at[k],
-            send_sem=s2.at[k],
-            recv_sem=r2.at[k],
-            device_id=(grp, day, dest),
+            src_ref=outbox.at[e],
+            dst_ref=inbox.at[e],
+            send_sem=s2.at[e],
+            recv_sem=r2.at[e],
+            device_id=(grp, day, flipped(me, e // most, n)),
             device_id_type=mesh_id,
         )
 
-    def start_two(k, _):
-        for r in range(most):
-            outbox[k, r] = resampled(k, r)
-        copy_two(k, lax.rem(me + k, n)).start()
-        return 0
-
-    lax.fori_loop(1, n, start_two, 0)
+    def start_two(e, _):
+        outbox[e] = resampled(e)
+        copy_two(e).start()
+        return 0
+
+    lax.fori_loop(most, total, start_two, 0)
 
     def copy_y(k):
         return pltpu.make_async_remote_copy(
@@ -307,10 +315,8 @@
         )
 
     def stage_a(k):
-        @pl.when(k > 0)
-        def _():
-            copy_two(k, lax.rem(me + k, n)).wait_recv()
-
+        if not isinstance(k, int) or k >= most:
+            copy_two(k).wait_recv()
         copy_y(k).start()
         if relay:
 
@@ -328,14 +334,14 @@
             def _():
                 copy_x(k, ybox).start()
 
-    def patches(k, r):
-        own = inbox[k, r].astype(F32)
+    def patches(at):
+        own = inbox[at].astype(F32)
         ore = own[:, :BLK]
         oim = own[:, BLK:]
         tops = []
         lows = []
         for box in (xbox, ybox):
-            oth = box[k, r].astype(F32)
+            oth = box[at].astype(F32)
             tre = oth[:, :BLK]
             tim = oth[:, BLK:]
             tops.append(ore * tre + oim * tim)
@@ -370,46 +376,64 @@
         weighted = jnp.concatenate(weighted, axis=0).astype(BF)
         back = mm(gbl_ref[...], turned(weighted)).astype(BF)
         done = mm(turned(back), gbr_ref[...]).astype(BF)
-        at = k * most + r
         for x in range(2):
             for c in range(2):
                 fil[at, x, c] = done[x * BLK : (x + 1) * BLK, c * BLK : (c + 1) * BLK]
 
     def stage_c(k):
         copy_x(k, inbox).wait_recv()
-        for r in range(most):
-            patches(k, r)
-
-    stage_a(0)
-    stage_a(1)
-    stage_b(0)
-
-    def step(k, _):
-        stage_a(k)
-        stage_b(k - 1)
-        stage_c(k - 2)
-        return 0
-
-    lax.fori_loop(2, n, step, 0)
-    stage_b(n - 1)
-
-    def last(k, _):
-        stage_c(k)
-        return 0
-
-    lax.fori_loop(n - 2, n, last, 0)
+        patches(k)
+
+    def many(stage, first, stop):
+        def one(k, _):
+            stage(k)
+            return 0
+
+        lax.fori_loop(first, stop, one, 0)
+
+    for e in range(most):
+        stage_a(e)
+    many(stage_a, most, 4)
+    many(stage_b, 0, 2)
+    many(stage_a, 4, 6)
+    many(stage_b, 2, 4)
+    many(stage_a, 6, 8)
+
+    def opening(e, _):
+        stage_c(e)
+        stage_b(e + 4)
+        return 0
+
+    lax.fori_loop(0, 2, opening, 0)
+    stage_b(6)
+
+    def step(e, _):
+        stage_c(e - 6)
+        stage_b(e - 1)
+        stage_a(e)
+        return 0
+
+    lax.fori_loop(8, total, step, 0)
+    many(stage_c, total - 6, total - 3)
+    stage_b(total - 1)
+    many(stage_c, total - 3, total)
 
     def drain(k, _):
-        @pl.when(k > 0)
-        def _():
-            copy_one(k).wait_send()
-            copy_two(k, lax.rem(me + k, n)).wait_send()
-
         copy_y(k).wait_send()
         copy_x(k, inbox).wait_send()
         return 0
 
-    lax.fori_loop(0, n, drain, 0)
+    def drain_one(k, _):
+        copy_one(k).wait_send()
+        return 0
+
+    def drain_two(k, _):
+        copy_two(k).wait_send()
+        return 0
+
+    lax.fori_loop(1, n, drain_one, 0)
+    lax.fori_loop(most, total, drain_two, 0)
+    lax.fori_loop(0, total, drain, 0)
 
 
 def place(capacity, entry_ref, fil, out_ref, sems):
@@ -445,7 +469,7 @@
     ]
     smem = pl.BlockSpec(memory_space=pltpu.SMEM)
     vmem = pl.BlockSpec(memory_space=pltpu.VMEM)
-    box = pltpu.VMEM((n, most, BLK, 2 * BLK), BF)
+    box = pltpu.VMEM((n * most, BLK, 2 * BLK), BF)
     sems = pltpu.SemaphoreType.DMA((n,))
     filtered, entry = pl.pallas_call(
         functools.partial(kernel, n, dates, most, capacity),
@@ -467,9 +491,11 @@
             box,
             box,
             box,
-            *[sems] * 8,
+            sems,
+            sems,
+            *[pltpu.SemaphoreType.DMA((n * most,))] * 6,
         ],
-        compiler_params=pltpu.CompilerParams(collective_id=0, has_side_effects=True),
+        compiler_params=pltpu.CompilerParams(collective_id=0, has_side_effects=True, vmem_limit_bytes=(12 + n * most // 2) << 20),
     )(
         block_owner,
         block_slot,
@@ -485,6 +511,7 @@
         in_specs=[smem, vmem],
         out_specs=pl.BlockSpec(memory_space=pl.ANY),
         scratch_shapes=[pltpu.SemaphoreType.DMA((capacity,))],
+        compiler_params=pltpu.CompilerParams(vmem_limit_bytes=8 << 20),
     )(entry, filtered)
     return out[None]
 

time: 65.9 us -> 79.3 us (1.20)
  the two profiles are of different devices: /device:TPU:26 before, /device:TPU:2 now
where the time goes in v3:
time: 79.3 us; the launch traced here: 78.2 us
  Pallas kernels  68.1 us (86%)
  local copies, waits for them, and re-layouts  10.1 us (13%)
    pallas_call x1, Pallas kernels, body(): pl.pallas_call(functools.partial(kernel, n, dates, most, capacity), out_s...  66.1 us
    unnamed x24, local copies, waits for them, and re-layouts  10.1 us
    pallas_call x1, Pallas kernels, body(): pl.pallas_call(functools.partial(place, capacity), out_shape=jax.ShapeDty...  1.98 us

profile of v3, /device:TPU:2, one launch (start us, length us, event | category | flops | bytes accessed | tf_op | source)
XLA Modules:
  0.0 78.2 jit_solution(2843289670469124759)
XLA Ops:
  0.0 0.0 copy-start
  0.0 0.9 %copy-done = bf16[256,256]{1,0:T(8,128)(2,1)S(1)} copy-done((bf16[256,256]{1,0:T(8,128)(2,1)S(1)}, bf16[256,256]{1,0:T(8,128)(2,1)}, u32[]{:S(2)}) %copy-start) | copy-done | bytes 131096
  0.9 0.0 copy-start.1
  0.9 0.9 %copy-done.1 = bf16[256,256]{1,0:T(8,128)(2,1)S(1)} copy-done((bf16[256,256]{1,0:T(8,128)(2,1)S(1)}, bf16[256,256]{1,0:T(8,128)(2,1)}, u32[]{:S(2)}) %copy-start.1) | copy-done | bytes 131096
  1.8 0.0 copy-start.2
  1.8 1.0 %copy-done.2 = bf16[1,2,16,8192]{3,2,1,0:T(8,128)(2,1)S(1)} copy-done((bf16[1,2,16,8192]{3,2,1,0:T(8,128)(2,1)S(1)}, bf16[1,2,16,8192]{3,2,1,0:T(8,128)(2,1)}, u32[]{:S(2)}) %copy-start.2) | copy-done | bytes 524312
  2.9 0.0 copy-start.3
  2.9 1.0 %copy-done.3 = bf16[2,128,1024]{2,1,0:T(8,128)(2,1)S(1)} copy-done((bf16[2,128,1024]{2,1,0:T(8,128)(2,1)S(1)}, bf16[2,128,1024]{2,1,0:T(8,128)(2,1)}, u32[]{:S(2)}) %copy-start.3) | copy-done | bytes 524312
  3.9 0.0 copy-start.4
  3.9 0.9 %copy-done.4 = bf16[8,128,128]{2,1,0:T(8,128)(2,1)S(1)} copy-done((bf16[8,128,128]{2,1,0:T(8,128)(2,1)S(1)}, bf16[8,128,128]{2,1,0:T(8,128)(2,1)}, u32[]{:S(2)}) %copy-start.4) | copy-done | bytes 262168
  4.8 0.0 copy-start.5
  4.8 0.9 %copy-done.5 = bf16[256,256]{1,0:T(8,128)(2,1)S(1)} copy-done((bf16[256,256]{1,0:T(8,128)(2,1)S(1)}, bf16[256,256]{1,0:T(8,128)(2,1)}, u32[]{:S(2)}) %copy-start.5) | copy-done | bytes 131096
  5.7 0.0 copy-start.6
  5.8 0.8 %copy-done.6 = f32[2,8192]{1,0:T(2,128)S(1)} copy-done((f32[2,8192]{1,0:T(2,128)S(1)}, f32[2,8192]{1,0:T(2,128)}, u32[]{:S(2)}) %copy-start.6) | copy-done | bytes 65560
  6.6 0.0 copy-start.7
  6.6 0.8 %copy-done.7 = f32[2,64,128]{2,1,0:T(8,128)S(1)} copy-done((f32[2,64,128]{2,1,0:T(8,128)S(1)}, f32[2,64,128]{2,1,0:T(8,128)}, u32[]{:S(2)}) %copy-start.7) | copy-done | bytes 65560
  7.4 0.0 copy-start.8
  7.4 0.8 copy-done.8
  8.2 0.0 copy-start.9
  8.2 0.7 copy-done.9
  8.8 0.7 copy-done.10
  9.5 0.7 copy-done.11
  10.2 66.1 %shard_map.154 = (bf16[17,2,2,128,128]{4,3,2,1,0:T(8,128)(2,1)S(1)}, s32[16]{0:T(128)S(1)}) custom-call(s32[1,64]{1,0:T(1,128)S(1)} %copy-done.9, s32[1,64]{1,0:T(1,128)S(1)} %copy-done.10, s32[1,64]{1,0:T(1,128)S(1)} %copy-done.11, bf16[2,16,8192]{2,1,0:T(8,128)(2,1)S(1)} %bitcast.2, f32[2,8192]{1,0:T(2,128)S(1)} %copy-done.6, ...), custom_call_target="tpu_custom_call" | custom-call | tf_op jit(solution)/shard_map/pallas_call | solution.py:474
  76.2 2.0 %shard_map.155 = bf16[16,2,2,128,128]{4,3,2,1,0:T(8,128)(2,1)} custom-call(s32[16]{0:T(128)S(1)} %get-tuple-element.7.entry_ref, bf16[17,2,2,128,128]{4,3,2,1,0:T(8,128)(2,1)S(1)} %get-tuple-element.8.fil), custom_call_target="tpu_custom_call" | custom-call | tf_op jit(solution)/shard_map/pallas_call | solution.py:508
  (2 shorter events, 0.0 us)
Async XLA Ops:
  0.0 0.9 %copy-start = (bf16[256,256]{1,0:T(8,128)(2,1)S(1)}, bf16[256,256]{1,0:T(8,128)(2,1)}, u32[]{:S(2)}) copy-start(bf16[256,256]{1,0:T(8,128)(2,1)} %constant.16.clone.pb_ref.gfr_ref.gbl_ref) | copy-start | bytes 393220
  0.9 0.9 %copy-start.1 = (bf16[256,256]{1,0:T(8,128)(2,1)S(1)}, bf16[256,256]{1,0:T(8,128)(2,1)}, u32[]{:S(2)}) copy-start(bf16[256,256]{1,0:T(8,128)(2,1)} %constant.15.clone.pf_ref.gfl_ref.gbr_ref) | copy-start | bytes 393220
  1.8 1.0 %copy-start.2 = (bf16[1,2,16,8192]{3,2,1,0:T(8,128)(2,1)S(1)}, bf16[1,2,16,8192]{3,2,1,0:T(8,128)(2,1)}, u32[]{:S(2)}) copy-start(bf16[1,2,16,8192]{3,2,1,0:T(8,128)(2,1)} %param.16) | copy-start | bytes 1572868
  2.9 1.0 %copy-start.3 = (bf16[2,128,1024]{2,1,0:T(8,128)(2,1)S(1)}, bf16[2,128,1024]{2,1,0:T(8,128)(2,1)}, u32[]{:S(2)}) copy-start(bf16[2,128,1024]{2,1,0:T(8,128)(2,1)} %aref_ref.1) | copy-start | bytes 1572868
  3.9 0.9 %copy-start.4 = (bf16[8,128,128]{2,1,0:T(8,128)(2,1)S(1)}, bf16[8,128,128]{2,1,0:T(8,128)(2,1)}, u32[]{:S(2)}) copy-start(bf16[8,128,128]{2,1,0:T(8,128)(2,1)} %constant.17.clone.kt_ref) | copy-start | bytes 786436
  4.8 0.9 %copy-start.5 = (bf16[256,256]{1,0:T(8,128)(2,1)S(1)}, bf16[256,256]{1,0:T(8,128)(2,1)}, u32[]{:S(2)}) copy-start(bf16[256,256]{1,0:T(8,128)(2,1)} %constant.12.clone.t1_ref) | copy-start | bytes 393220
  5.7 0.8 %copy-start.6 = (f32[2,8192]{1,0:T(2,128)S(1)}, f32[2,8192]{1,0:T(2,128)}, u32[]{:S(2)}) copy-start(f32[2,8192]{1,0:T(2,128)} %rref_ref.1) | copy-start | bytes 196612
  6.6 0.8 %copy-start.7 = (f32[2,64,128]{2,1,0:T(8,128)S(1)}, f32[2,64,128]{2,1,0:T(8,128)}, u32[]{:S(2)}) copy-start(f32[2,64,128]{2,1,0:T(8,128)} %constant.13.clone.tw_ref) | copy-start | bytes 196612
  7.4 0.8 copy-start.8
  8.2 0.7 copy-start.9
  8.8 0.7 copy-start.10
  9.5 0.7 copy-start.11

commit v4 on v3

--- a/solution.py
+++ b/solution.py
@@ -75,6 +75,37 @@
     dates,
     most,
     capacity,
+    owner_hbm,
+    slot_hbm,
+    kinds_hbm,
+    echo_hbm,
+    rref_hbm,
+    aref_hbm,
+    t1_hbm,
+    tw_hbm,
+    w2_hbm,
+    pf_hbm,
+    pb_hbm,
+    kt_hbm,
+    gfl_hbm,
+    gfr_hbm,
+    gbl_hbm,
+    gbr_hbm,
+    fil_hbm,
+    entry_ref,
+    fil,
+    src_ref,
+    kind_ref,
+    lhs,
+    mat,
+    snd,
+    cols,
+    blocks,
+    outbox,
+    inbox,
+    ybox,
+    xbox,
+    sw,
     owner_ref,
     slot_ref,
     kinds_ref,
@@ -91,19 +122,7 @@
     gfr_ref,
     gbl_ref,
     gbr_ref,
-    fil,
-    entry_ref,
-    src_ref,
-    kind_ref,
-    lhs,
-    mat,
-    snd,
-    cols,
-    blocks,
-    outbox,
-    inbox,
-    ybox,
-    xbox,
+    s0,
     s1,
     r1,
     s2,
@@ -113,6 +132,31 @@
     sx,
     rx,
 ):
+    loads = [
+        pltpu.make_async_copy(source, held, s0.at[at])
+        for at, (source, held) in enumerate(
+            [
+                (echo_hbm, echo_ref),
+                (rref_hbm, rref_ref),
+                (t1_hbm, t1_ref),
+                (tw_hbm, tw_ref),
+                (w2_hbm, w2_ref),
+                (owner_hbm, owner_ref),
+                (slot_hbm, slot_ref),
+                (kinds_hbm, kinds_ref),
+                (pf_hbm, pf_ref),
+                (aref_hbm, aref_ref),
+                (pb_hbm, pb_ref),
+                (kt_hbm, kt_ref),
+                (gfl_hbm, gfl_ref),
+                (gfr_hbm, gfr_ref),
+                (gbl_hbm, gbl_ref),
+                (gbr_hbm, gbr_ref),
+            ]
+        )
+    ]
+    for load in loads:
+        load.start()
     me = lax.axis_index("shard")
     day = lax.axis_index("date")
     grp = lax.axis_index("grp")
@@ -147,6 +191,8 @@
     mine = tiles // n
     wide = n * pulses
 
+    loads[0].wait()
+    loads[1].wait()
     real = echo_ref[0].astype(F32)
     imag = echo_ref[1].astype(F32)
     rre = rref_ref[0:1, :]
@@ -160,6 +206,8 @@
         parts = [both[x * inner : (x + 1) * inner] for x in range(low)]
         lhs[p * inner : (p + 1) * inner, :] = jnp.concatenate(parts, axis=1).astype(BF)
 
+    for load in loads[2:5]:
+        load.wait()
     twc = tw_ref[0]
     tws = tw_ref[1]
     group = 4
@@ -213,6 +261,9 @@
     lax.fori_loop(1, n, start_one, 0)
     cols[:, :, pl.ds(me * pulses, pulses)] = snd[:, pl.ds(me * mine, mine)]
 
+    for load in loads[5:]:
+        load.wait()
+
     def sources(k, _):
         dest = flipped(me, k, n)
         seen = jnp.int32(0)
@@ -244,6 +295,11 @@
     for q in range(capacity):
         entry_ref[q] = held[q]
     fil[n * most] = jnp.zeros_like(fil[n * most])
+
+    def write(e):
+        return pltpu.make_async_copy(fil.at[e], fil_hbm.at[e], sw.at[e])
+
+    write(n * most).start()
     lax.fori_loop(1, n, end_one, 0)
 
     rows_of = wide // BLK
@@ -383,6 +439,7 @@
     def stage_c(k):
         copy_x(k, inbox).wait_recv()
         patches(k)
+        write(k).start()
 
     def many(stage, first, stop):
         def one(k, _):
@@ -394,27 +451,29 @@
     for e in range(most):
         stage_a(e)
     many(stage_a, most, 4)
-    many(stage_b, 0, 2)
-    many(stage_a, 4, 6)
-    many(stage_b, 2, 4)
-    many(stage_a, 6, 8)
 
     def opening(e, _):
+        stage_a(e + 4)
+        stage_b(e)
+        return 0
+
+    lax.fori_loop(0, 4, opening, 0)
+
+    def middle(e, _):
         stage_c(e)
         stage_b(e + 4)
         return 0
 
-    lax.fori_loop(0, 2, opening, 0)
-    stage_b(6)
+    lax.fori_loop(0, 3, middle, 0)
 
     def step(e, _):
-        stage_c(e - 6)
+        stage_a(e)
         stage_b(e - 1)
-        stage_a(e)
+        stage_c(e - 5)
         return 0
 
     lax.fori_loop(8, total, step, 0)
-    many(stage_c, total - 6, total - 3)
+    many(stage_c, total - 5, total - 3)
     stage_b(total - 1)
     many(stage_c, total - 3, total)
 
@@ -435,15 +494,27 @@
     lax.fori_loop(most, total, drain_two, 0)
     lax.fori_loop(0, total, drain, 0)
 
-
-def place(capacity, entry_ref, fil, out_ref, sems):
-    def copy(q):
-        return pltpu.make_async_copy(fil.at[entry_ref[q]], out_ref.at[q], sems.at[q])
+    def written(k, _):
+        write(k).wait()
+        return 0
+
+    lax.fori_loop(0, total + 1, written, 0)
+
+
+def place(capacity, entry_ref, fil, out_ref, held, near, far):
+    def take(q):
+        return pltpu.make_async_copy(fil.at[entry_ref[q]], held.at[q], near.at[q])
+
+    def give(q):
+        return pltpu.make_async_copy(held.at[q], out_ref.at[q], far.at[q])
 
     for q in range(capacity):
-        copy(q).start()
+        take(q).start()
     for q in range(capacity):
-        copy(q).wait()
+        take(q).wait()
+        give(q).start()
+    for q in range(capacity):
+        give(q).wait()
 
 
 def body(dates, echo_spectra, range_reference, azimuth_reference, block_owner, block_slot, kernel_index):
@@ -468,18 +539,22 @@
         right_table(BLK, 1),
     ]
     smem = pl.BlockSpec(memory_space=pltpu.SMEM)
-    vmem = pl.BlockSpec(memory_space=pltpu.VMEM)
+    hbm = pl.BlockSpec(memory_space=pl.ANY)
     box = pltpu.VMEM((n * most, BLK, 2 * BLK), BF)
     sems = pltpu.SemaphoreType.DMA((n,))
+    tables = [jnp.asarray(t) for t in tables]
+    operands = [block_owner, block_slot, kernel_index, echo, range_reference, azimuth_reference]
+    operands += tables
     filtered, entry = pl.pallas_call(
         functools.partial(kernel, n, dates, most, capacity),
         out_shape=(
             jax.ShapeDtypeStruct((n * most + 1, 2, 2, BLK, BLK), BF),
             jax.ShapeDtypeStruct((capacity,), jnp.int32),
         ),
-        in_specs=[smem] * 3 + [vmem] * 13,
-        out_specs=(vmem, smem),
+        in_specs=[hbm] * 16,
+        out_specs=(hbm, smem),
         scratch_shapes=[
+            pltpu.VMEM((n * most + 1, 2, 2, BLK, BLK), BF),
             pltpu.SMEM((n * most,), jnp.int32),
             pltpu.SMEM((n * most,), jnp.int32),
             pltpu.VMEM((pulses * inner, 2 * BLK), BF),
@@ -491,27 +566,27 @@
             box,
             box,
             box,
+            pltpu.SemaphoreType.DMA((n * most + 1,)),
+            *[pltpu.SMEM(x.shape, x.dtype) for x in operands[:3]],
+            *[pltpu.VMEM(x.shape, x.dtype) for x in operands[3:]],
+            pltpu.SemaphoreType.DMA((len(operands),)),
             sems,
             sems,
             *[pltpu.SemaphoreType.DMA((n * most,))] * 6,
         ],
-        compiler_params=pltpu.CompilerParams(collective_id=0, has_side_effects=True, vmem_limit_bytes=(12 + n * most // 2) << 20),
+        compiler_params=pltpu.CompilerParams(collective_id=0, has_side_effects=True),
     )(
-        block_owner,
-        block_slot,
-        kernel_index,
-        echo,
-        range_reference,
-        azimuth_reference,
-        *[jnp.asarray(t) for t in tables],
+        *operands
     )
     out = pl.pallas_call(
         functools.partial(place, capacity),
         out_shape=jax.ShapeDtypeStruct((capacity, 2, 2, BLK, BLK), BF),
-        in_specs=[smem, vmem],
+        in_specs=[smem, hbm],
         out_specs=pl.BlockSpec(memory_space=pl.ANY),
-        scratch_shapes=[pltpu.SemaphoreType.DMA((capacity,))],
-        compiler_params=pltpu.CompilerParams(vmem_limit_bytes=8 << 20),
+        scratch_shapes=[
+            pltpu.VMEM((capacity, 2, 2, BLK, BLK), BF),
+            *[pltpu.SemaphoreType.DMA((capacity,))] * 2,
+        ],
     )(entry, filtered)
     return out[None]
 

time: 79.3 us -> 64.2 us (0.81)
  local copies, waits for them, and re-layouts: 10.1 us -> 0 us
  Pallas kernels: 68.1 us -> 63.4 us
    unnamed x24 -> x0, local copies, waits for them, and re-layouts: 10.1 us -> none
    pallas_call x1, Pallas kernels: 66.1 us -> 58.9 us  [body(): pl.pallas_call(functools.partial(kernel, n, dates, most, capacity), out_s...]
    pallas_call x1, Pallas kernels: 1.98 us -> 4.43 us  [body(): pl.pallas_call(functools.partial(place, capacity), out_shape=jax.ShapeDty...]
where the time goes in v4:
time: 64.2 us; the launch traced here: 63.4 us
  Pallas kernels  63.4 us (99%)
    pallas_call x1, Pallas kernels, body(): pl.pallas_call(functools.partial(kernel, n, dates, most, capacity), out_s...  58.9 us
    pallas_call x1, Pallas kernels, body(): pl.pallas_call(functools.partial(place, capacity), out_shape=jax.ShapeDty...  4.43 us

profile of v4, /device:TPU:2, one launch (start us, length us, event | category | flops | bytes accessed | tf_op | source)
XLA Modules:
  0.0 63.4 jit_solution(9253721877639085334)
XLA Ops:
  0.0 58.9 %shard_map.154 = (bf16[17,2,2,128,128]{4,3,2,1,0:T(8,128)(2,1)}, s32[16]{0:T(128)}) custom-call(s32[1,64]{1,0:T(1,128)} %owner_hbm.1, s32[1,64]{1,0:T(1,128)} %slot_hbm.1, s32[1,64]{1,0:T(1,128)} %kinds_hbm.1, bf16[2,16,8192]{2,1,0:T(8,128)(2,1)} %bitcast.2, f32[2,8192]{1,0:T(2,128)} %rref_hbm.1, bf16[2,128,1024]{2,1,0:T(8,128)(2,1)} %aref_hbm.1, ...), custom_call_target="tpu_custom_call" | custom-call | tf_op jit(solution)/shard_map/pallas_call | solution.py:548
  58.9 4.4 %shard_map.155 = bf16[16,2,2,128,128]{4,3,2,1,0:T(8,128)(2,1)} custom-call(s32[16]{0:T(128)} %get-tuple-element.7.entry_ref, bf16[17,2,2,128,128]{4,3,2,1,0:T(8,128)(2,1)} %get-tuple-element.8.fil), custom_call_target="tpu_custom_call" | custom-call | tf_op jit(solution)/shard_map/pallas_call | solution.py:581

commit v5 on v3

--- a/solution.py
+++ b/solution.py
@@ -91,8 +91,9 @@
     gfr_ref,
     gbl_ref,
     gbr_ref,
+    fil_hbm,
+    entry_ref,
     fil,
-    entry_ref,
     src_ref,
     kind_ref,
     lhs,
@@ -104,6 +105,7 @@
     inbox,
     ybox,
     xbox,
+    sw,
     s1,
     r1,
     s2,
@@ -244,6 +246,11 @@
     for q in range(capacity):
         entry_ref[q] = held[q]
     fil[n * most] = jnp.zeros_like(fil[n * most])
+
+    def write(e):
+        return pltpu.make_async_copy(fil.at[e], fil_hbm.at[e], sw.at[e])
+
+    write(n * most).start()
     lax.fori_loop(1, n, end_one, 0)
 
     rows_of = wide // BLK
@@ -383,6 +390,7 @@
     def stage_c(k):
         copy_x(k, inbox).wait_recv()
         patches(k)
+        write(k).start()
 
     def many(stage, first, stop):
         def one(k, _):
@@ -394,29 +402,33 @@
     for e in range(most):
         stage_a(e)
     many(stage_a, most, 4)
-    many(stage_b, 0, 2)
-    many(stage_a, 4, 6)
-    many(stage_b, 2, 4)
-    many(stage_a, 6, 8)
 
     def opening(e, _):
+        stage_a(e + 4)
+        stage_b(e)
+        return 0
+
+    lax.fori_loop(0, 4, opening, 0)
+
+    def middle(e, _):
         stage_c(e)
         stage_b(e + 4)
         return 0
 
-    lax.fori_loop(0, 2, opening, 0)
-    stage_b(6)
+    lax.fori_loop(0, 2, middle, 0)
+    stage_c(2)
 
     def step(e, _):
-        stage_c(e - 6)
-        stage_b(e - 1)
         stage_a(e)
+        stage_b(e - 2)
+        stage_c(e - 5)
         return 0
 
     lax.fori_loop(8, total, step, 0)
-    many(stage_c, total - 6, total - 3)
+    stage_b(total - 2)
+    stage_c(total - 5)
     stage_b(total - 1)
-    many(stage_c, total - 3, total)
+    many(stage_c, total - 4, total)
 
     def drain(k, _):
         copy_y(k).wait_send()
@@ -434,6 +446,12 @@
     lax.fori_loop(1, n, drain_one, 0)
     lax.fori_loop(most, total, drain_two, 0)
     lax.fori_loop(0, total, drain, 0)
+
+    def written(k, _):
+        write(k).wait()
+        return 0
+
+    lax.fori_loop(0, total + 1, written, 0)
 
 
 def place(capacity, entry_ref, fil, out_ref, sems):
@@ -469,8 +487,12 @@
     ]
     smem = pl.BlockSpec(memory_space=pltpu.SMEM)
     vmem = pl.BlockSpec(memory_space=pltpu.VMEM)
+    hbm = pl.BlockSpec(memory_space=pl.ANY)
     box = pltpu.VMEM((n * most, BLK, 2 * BLK), BF)
     sems = pltpu.SemaphoreType.DMA((n,))
+    tables = [jnp.asarray(t) for t in tables]
+    operands = [block_owner, block_slot, kernel_index, echo, range_reference, azimuth_reference]
+    operands += tables
     filtered, entry = pl.pallas_call(
         functools.partial(kernel, n, dates, most, capacity),
         out_shape=(
@@ -478,8 +500,9 @@
             jax.ShapeDtypeStruct((capacity,), jnp.int32),
         ),
         in_specs=[smem] * 3 + [vmem] * 13,
-        out_specs=(vmem, smem),
+        out_specs=(hbm, smem),
         scratch_shapes=[
+            pltpu.VMEM((n * most + 1, 2, 2, BLK, BLK), BF),
             pltpu.SMEM((n * most,), jnp.int32),
             pltpu.SMEM((n * most,), jnp.int32),
             pltpu.VMEM((pulses * inner, 2 * BLK), BF),
@@ -491,19 +514,14 @@
             box,
             box,
             box,
+            pltpu.SemaphoreType.DMA((n * most + 1,)),
             sems,
             sems,
             *[pltpu.SemaphoreType.DMA((n * most,))] * 6,
         ],
-        compiler_params=pltpu.CompilerParams(collective_id=0, has_side_effects=True, vmem_limit_bytes=(12 + n * most // 2) << 20),
+        compiler_params=pltpu.CompilerParams(collective_id=0, has_side_effects=True),
     )(
-        block_owner,
-        block_slot,
-        kernel_index,
-        echo,
-        range_reference,
-        azimuth_reference,
-        *[jnp.asarray(t) for t in tables],
+        *operands
     )
     out = pl.pallas_call(
         functools.partial(place, capacity),
@@ -511,7 +529,6 @@
         in_specs=[smem, vmem],
         out_specs=pl.BlockSpec(memory_space=pl.ANY),
         scratch_shapes=[pltpu.SemaphoreType.DMA((capacity,))],
-        compiler_params=pltpu.CompilerParams(vmem_limit_bytes=8 << 20),
     )(entry, filtered)
     return out[None]
 

time: 79.3 us -> 59.7 us (0.75)
  local copies, waits for them, and re-layouts: 10.1 us -> 0 us
  Pallas kernels: 68.1 us -> 58.6 us
    pallas_call x1, Pallas kernels: 66.1 us -> 55.5 us  [body(): pl.pallas_call(functools.partial(kernel, n, dates, most, capacity), out_s...]
    unnamed x24 -> x0, local copies, waits for them, and re-layouts: 10.1 us -> none
    pallas_call x1, Pallas kernels: 1.98 us -> 3.08 us  [body(): pl.pallas_call(functools.partial(place, capacity), out_shape=jax.ShapeDty...]
where the time goes in v5:
time: 59.7 us; the launch traced here: 58.6 us
  Pallas kernels  58.6 us (98%)
    pallas_call x1, Pallas kernels, body(): pl.pallas_call(functools.partial(kernel, n, dates, most, capacity), out_s...  55.5 us
    pallas_call x1, Pallas kernels, body(): pl.pallas_call(functools.partial(place, capacity), out_shape=jax.ShapeDty...  3.08 us

profile of v5, /device:TPU:2, one launch (start us, length us, event | category | flops | bytes accessed | tf_op | source)
XLA Modules:
  0.0 58.6 jit_solution(8563641768106785581)
XLA Ops:
  0.0 55.5 %shard_map.154 = (bf16[17,2,2,128,128]{4,3,2,1,0:T(8,128)(2,1)}, s32[16]{0:T(128)}) custom-call(s32[1,64]{1,0:T(1,128)} %owner_ref.1, s32[1,64]{1,0:T(1,128)} %slot_ref.1, s32[1,64]{1,0:T(1,128)} %kinds_ref.1, bf16[2,16,8192]{2,1,0:T(8,128)(2,1)} %bitcast.2, f32[2,8192]{1,0:T(2,128)} %rref_ref.1, bf16[2,128,1024]{2,1,0:T(8,128)(2,1)} %aref_ref.1, ...), custom_call_target="tpu_custom_call" | custom-call | tf_op jit(solution)/shard_map/pallas_call | solution.py:496
  55.5 3.1 %shard_map.155 = bf16[16,2,2,128,128]{4,3,2,1,0:T(8,128)(2,1)} custom-call(s32[16]{0:T(128)} %get-tuple-element.7.entry_ref, bf16[17,2,2,128,128]{4,3,2,1,0:T(8,128)(2,1)} %get-tuple-element.8.fil), custom_call_target="tpu_custom_call" | custom-call | tf_op jit(solution)/shard_map/pallas_call | solution.py:526
